TPU v7x, 32 devices: a whole 2x2x4 slice. The times are simulated.
32 devices in a mesh: gx: 8 (over z, x), gy: 4 (over y, core).
Axes of the slice: x: 2, y: 2, z: 4, core: 2. Of those that a mesh axis runs over, the one named last changes fastest.
Arguments:
- reference_scan: bfloat16 [128, 128, 2048], P('gx', 'gy'), may hold values from -6 to 6
- ref_gradient: bfloat16 [3, 128, 128, 2048], P(None, 'gx', 'gy'), may hold values from -6 to 6
- deformed_scan: bfloat16 [128, 128, 2048], P('gx', 'gy'), may hold values from -6 to 6
- interp_weights: bfloat16 [128, 128, 2048], P('gx', 'gy'), may hold values from 0 to 1
- sample_mask: int32 [128, 128, 2048], P('gx', 'gy'), may hold values from 0 to 1, as said below
- block_list: int32 [8, 16384], P('gx', 'gy'), may hold values from -1 to 8191, as said below
- offsets: int32 [2, 128, 128, 4], P(None, 'gx', 'gy'), may hold values from -4 to 4, as said below
Outputs:
- increment: float32 [3, 128, 128, 5], P(None, 'gx', 'gy')
- cg_residual: float32 [3, 128, 128, 5], P(None, 'gx', 'gy')
Inputs may be any that keep to these rules, and one draw needn't show every extreme that they name: sample_mask is 0 in every block of 128 voxels that its device's block_list does not name. `block_list`: each device's 4096 entries are first distinct local block indices, then -1 to the end; some device names exactly 4096 blocks. `offsets`: both ends of the range occur.
All inputs are finite; a program needn't handle non-finite values.
Results may differ from a plain program's by a relative error of at most 0.0045.
Values may be sent and summed in bfloat16 or wider, within the bound.
A program may use at most 320 MiB of HBM per device.

v0:
```python
import jax
import jax.numpy as jnp
from jax import lax
from jax.sharding import PartitionSpec as P

BOUND = 4
ITERS = 3
tikhonov = 8.0


def extended(value, sides, width):
    for axis, dim in sides:
        devices, length = (lax.axis_size(axis), value.shape[dim])
        up = [(i, (i + 1) % devices) for i in range(devices - 1)]
        down = [(j, i) for i, j in up]
        last = lax.slice_in_dim(value, length - width, length, axis=dim)
        first = lax.slice_in_dim(value, 0, width, axis=dim)
        before = lax.ppermute(last, axis, up)
        after = lax.ppermute(first, axis, down)
        value = jnp.concatenate([before, value, after], axis=dim)
    return value


def from_behind(block, axis, distance):
    devices = range(lax.axis_size(axis))
    route = [(i - distance, i) for i in devices if i - distance in devices]
    return lax.ppermute(block, axis, route)


def shape_table():
    voxel = jnp.arange(512)
    coords = [
        ((voxel // 64).astype(jnp.float32) + 0.5) / 8.0,
        ((voxel // 8 % 8).astype(jnp.float32) + 0.5) / 8.0,
        ((voxel % 8).astype(jnp.float32) + 0.5) / 8.0,
    ]
    rows = []
    for node in range(8):
        bits = [node >> 2 & 1, node >> 1 & 1, node & 1]
        value = jnp.ones((512,), jnp.float32)
        for axis_pos in range(3):
            value = value * (coords[axis_pos] if bits[axis_pos] else 1.0 - coords[axis_pos])
        rows.append(value)
    return jnp.transpose(jnp.stack(rows).reshape(8, 4, 128), (1, 0, 2))


def block_terms(grad_rows, resid_rows, mask_rows, kinds, table):
    onehot = (kinds[:, None] == jnp.arange(4)[None, :]).astype(jnp.float32)
    shapes = jnp.einsum("bk,knv->bnv", onehot, table, precision=lax.Precision.HIGHEST)
    product = shapes[:, :, None, :] * grad_rows[:, None, :, :].astype(jnp.float32)
    jacobian = product.reshape(kinds.shape[0], 24, 128).astype(jnp.bfloat16)
    weighted = jacobian * mask_rows[:, None, :]
    hessian = jnp.einsum("bdv,bev->bde", weighted, jacobian, preferred_element_type=jnp.float32)
    gradient = jnp.einsum("bdv,bv->bd", weighted, resid_rows, preferred_element_type=jnp.float32)
    return (hessian, gradient)


def run_groups(grad_rows, resid_rows, mask_rows, kinds, table):
    count = kinds.shape[0]
    groups = 4
    packed = (
        grad_rows.reshape((groups, count // groups) + grad_rows.shape[1:]),
        resid_rows.reshape(groups, count // groups, 128),
        mask_rows.reshape(groups, count // groups, 128),
        kinds.reshape(groups, count // groups),
    )
    hessian, gradient = lax.map(
        lambda parts: block_terms(parts[0], parts[1], parts[2], parts[3], table), packed
    )
    return (hessian.reshape(count, 24, 24), gradient.reshape(count, 24))


def per_device(
    reference_scan, ref_gradient, deformed_scan, interp_weights, sample_mask, block_list, offsets
):
    tile_x, tile_y, column = reference_scan.shape
    elem_depth = column // 512
    padded = extended(deformed_scan, (("gx", 0), ("gy", 1)), BOUND + 1)
    margin = BOUND + 1
    span_y = padded.shape[1]
    flat_scan = padded.reshape(padded.shape[0] * span_y, elem_depth, 512)
    pos_x = jnp.arange(tile_x)[:, None, None]
    pos_y = jnp.arange(tile_y)[None, :, None]
    source = (pos_x + offsets[0] + margin) * span_y + pos_y + offsets[1] + margin
    layer = jnp.broadcast_to(jnp.arange(elem_depth)[None, None, :], source.shape)
    near = flat_scan[source, layer].astype(jnp.float32)
    far = flat_scan[source + span_y, layer].astype(jnp.float32)
    weights = interp_weights.reshape(tile_x, tile_y, elem_depth, 512).astype(jnp.float32)
    warped = weights * near + (1.0 - weights) * far
    residual_image = (
        reference_scan.reshape(tile_x, tile_y, elem_depth, 512).astype(jnp.float32) - warped
    ).astype(jnp.bfloat16)
    local_blocks = tile_x * tile_y * elem_depth * 4
    elements = local_blocks // 4
    grad_blocks = jnp.moveaxis(ref_gradient.reshape(3, local_blocks, 128), 0, 1)
    resid_blocks = residual_image.reshape(local_blocks, 128)
    mask_blocks = sample_mask.reshape(local_blocks, 128)
    entries = block_list.reshape(-1)
    listed = entries >= 0
    safe = jnp.maximum(entries, 0)
    table = shape_table()
    marks = jnp.zeros((local_blocks,), jnp.bfloat16).at[safe].add(listed.astype(jnp.bfloat16))
    mask_rows = mask_blocks.astype(jnp.bfloat16) * marks[:, None]
    hessian, gradient = run_groups(
        grad_blocks, resid_blocks, mask_rows, jnp.arange(local_blocks) % 4, table
    )
    elem_hess = hessian.reshape(elements, 4, 24, 24).sum(axis=1)
    elem_load = gradient.reshape(elements, 4, 24).sum(axis=1)
    stiffness = jnp.transpose(elem_hess, (1, 2, 0))
    loads = jnp.transpose(elem_load, (1, 0))

    def spread(field):
        upper_x = from_behind(field[:, :1], "gx", -1)
        wide = jnp.concatenate([field, upper_x], axis=1)
        upper_y = from_behind(wide[:, :, :1], "gy", -1)
        wide = jnp.concatenate([wide, upper_y], axis=2)
        pieces = []
        for node in range(8):
            i_bit, j_bit, l_bit = (node >> 2 & 1, node >> 1 & 1, node & 1)
            pieces.append(
                wide[:, i_bit : i_bit + tile_x, j_bit : j_bit + tile_y, l_bit : l_bit + elem_depth]
            )
        return jnp.stack(pieces).reshape(24, elements)

    def collect(values):
        parts = values.reshape(8, 3, tile_x, tile_y, elem_depth)
        total = jnp.zeros((3, tile_x + 1, tile_y + 1, elem_depth + 1), jnp.float32)
        for node in range(8):
            i_bit, j_bit, l_bit = (node >> 2 & 1, node >> 1 & 1, node & 1)
            total = total + jnp.pad(
                parts[node], ((0, 0), (i_bit, 1 - i_bit), (j_bit, 1 - j_bit), (l_bit, 1 - l_bit))
            )
        passed_y = from_behind(total[:, :, tile_y:], "gy", 1)
        total = total[:, :, :tile_y].at[:, :, 0:1].add(passed_y)
        passed_x = from_behind(total[:, tile_x:], "gx", 1)
        return total[:, :tile_x].at[:, 0:1].add(passed_x)

    def operate(field):
        images = jnp.einsum("nzr,zr->nr", stiffness, spread(field), precision=lax.Precision.HIGHEST)
        return collect(images) + tikhonov * field

    def two_products(vector, image):
        return lax.psum((jnp.sum(vector * vector), jnp.sum(vector * image)), ("gx", "gy"))

    rhs = collect(loads)
    increment = jnp.zeros_like(rhs)
    cg_residual = rhs
    image = operate(cg_residual)
    norm_now, product = two_products(cg_residual, image)
    step_size = norm_now / product
    direction, along = (cg_residual, image)
    for sweep in range(ITERS):
        increment = increment + step_size * direction
        cg_residual = cg_residual - step_size * along
        if sweep + 1 < ITERS:
            image = operate(cg_residual)
            norm_next, product = two_products(cg_residual, image)
            factor = norm_next / norm_now
            step_size = norm_next / (product - factor * norm_next / step_size)
            direction = cg_residual + factor * direction
            along = image + factor * along
            norm_now = norm_next
    return (increment, cg_residual)


def solution(mesh):
    return jax.shard_map(
        per_device,
        mesh=mesh,
        in_specs=(
            P("gx", "gy", None),
            P(None, "gx", "gy", None),
            P("gx", "gy", None),
            P("gx", "gy", None),
            P("gx", "gy", None),
            P("gx", "gy"),
            P(None, "gx", "gy", None),
        ),
        out_specs=(P(None, "gx", "gy", None), P(None, "gx", "gy", None)),
        check_vma=False,
    )
```

profile of v0, /device:TPU:0, one launch (start us, length us, event | category | flops | bytes accessed | tf_op | source)
XLA Modules:
  0.0 903.4 jit_solution(9337056668083446105)
XLA Ops:
  3.0 5.7 collective-permute-start
  13.6 4.5 reshape.733
  18.1 4.5 reshape.734
  22.7 4.0 convert_element_type.286
  26.6 4.2 convert_element_type.287
  30.8 29.1 %scatter_custom_fusion = bf16[8192]{0:T(1024)(128)(2,1)S(1)} fusion(s32[4096]{0:T(1024)S(1)} %bitcast.232, bf16[4096]{0:T(1024)(128)(2,1)S(1)} %fusion.63, bf16[]{:T(256)} %constant.278.clone.1), kind=kCustom, calls=%fused_computation.157 | custom fusion | flops 4096 | bytes 16386 | tf_op jit(solution)/shard_map/scatter-add | solution.py:102
  59.9 10.5 %reshape.725 = bf16[3,8192,128]{2,1,0:T(8,128)(2,1)} reshape(bf16[3,16,32,2048]{3,2,1,0:T(8,128)(2,1)} %param.26) | data formatting | bytes 12582912 | tf_op jit(solution)/shard_map/reshape | solution.py:95
  81.0 6.1 pad_maximum_fusion
  87.1 4.8 copy.263
  91.9 10.6 %reshape.727 = bf16[1092,4,512]{2,1,0:T(4,128)(2,1)} reshape(bf16[26,42,2048]{2,1,0:T(8,128)(2,1)} %copy.263) | data formatting | bytes 8945664 | tf_op jit(solution)/shard_map/reshape | solution.py:81
  102.4 26.4 %gather_fusion = bf16[2048,512]{1,0:T(8,128)(2,1)S(1)} fusion(bf16[1092,4,512]{2,1,0:T(4,128)(2,1)} %reshape.727, s32[2048]{0:T(1024)S(1)} %reshape.737), kind=kCustom, calls=%fused_computation | custom fusion | bytes 4210688 | tf_op jit(solution)/shard_map/gather | solution.py:86
  131.7 26.4 %gather_fusion.1 = bf16[2048,512]{1,0:T(8,128)(2,1)S(1)} fusion(bf16[1092,4,512]{2,1,0:T(4,128)(2,1)} %reshape.727, s32[2048]{0:T(1024)S(1)} %reshape.743), kind=kCustom, calls=%fused_computation.1 | custom fusion | bytes 4210688 | tf_op jit(solution)/shard_map/gather | solution.py:87
  161.0 6.7 subtract_convert_fusion
  167.7 264.3 %while.20 = (s32[]{:T(128)}, f32[4,2048,24,24]{3,2,1,0:T(8,128)}, f32[4,2048,24]{1,2,0:T(8,128)}, s32[4,2048]{1,0:T(4,128)S(1)}, f32[4,8,128]{2,0,1:T(4,128)S(1)...) while((s32[]{:T(128)}, f32[4,2048,24,24]{3,2,1,0:T(8,128)}, ...), condition=%wide.region_2.3_spmd, body=%wide.region_1.2_spmd.sunk | while | flops 434905088 | bytes 179807376 | solution.py:67
  167.9 3.5 fusion.101
  173.0 3.4 multiply_convert_fusion.2
  177.9 6.8 broadcast_multiply_fusion.3
  184.7 27.1 %bitcast_dynamic-update-slice_fusion.4 = f32[4,2048,24,24]{3,2,1,0:T(8,128)} fusion(f32[4,2048,24,24]{3,2,1,0:T(8,128)} %get-tuple-element.346, s32[]{:T(128)} %get-tuple-element.345, bf16[2048,24,128]{2,0,1:T(8,128)(2,1)} %bitcast.212, bf16[2048,24,128]{2,0,1:T(8,128)(2,1)} %broadcast_multiply_fusion.3), kind=kOutput, calls=%fused_computation.3.clone.1 | convolution fusion | flops 301989888 | bytes 50332160 | tf_op jit(solution)/shard_map/while/body/eval_jaxpr/bdv,bev->bde/dot_general | solution.py:53
  211.8 20.8 %fusion.102 = f32[2048,1,24]{2,1,0:T(1,128)S(1)} fusion(bf16[2048,24,128]{2,0,1:T(8,128)(2,1)} %broadcast_multiply_fusion.3, bf16[2048,128,1]{1,0,2:T(8,128)(2,1)S(1)} %dynamic-slice_bitcast_fusion.5), kind=kOutput, calls=%fused_computation.7.clone.1 | convolution fusion | flops 12582912 | bytes 13303808 | tf_op jit(solution)/shard_map/while/body/eval_jaxpr/bdv,bv->bd/dot_general | solution.py:54
  233.8 3.5 fusion.101
  238.9 3.4 multiply_convert_fusion.2
  243.8 6.8 broadcast_multiply_fusion.3
  250.6 27.0 %bitcast_dynamic-update-slice_fusion.4 = f32[4,2048,24,24]{3,2,1,0:T(8,128)} fusion(f32[4,2048,24,24]{3,2,1,0:T(8,128)} %get-tuple-element.346, s32[]{:T(128)} %get-tuple-element.345, bf16[2048,24,128]{2,0,1:T(8,128)(2,1)} %bitcast.212, bf16[2048,24,128]{2,0,1:T(8,128)(2,1)} %broadcast_multiply_fusion.3), kind=kOutput, calls=%fused_computation.3.clone.1 | convolution fusion | flops 301989888 | bytes 50332160 | tf_op jit(solution)/shard_map/while/body/eval_jaxpr/bdv,bev->bde/dot_general | solution.py:53
  277.7 20.8 %fusion.102 = f32[2048,1,24]{2,1,0:T(1,128)S(1)} fusion(bf16[2048,24,128]{2,0,1:T(8,128)(2,1)} %broadcast_multiply_fusion.3, bf16[2048,128,1]{1,0,2:T(8,128)(2,1)S(1)} %dynamic-slice_bitcast_fusion.5), kind=kOutput, calls=%fused_computation.7.clone.1 | convolution fusion | flops 12582912 | bytes 13303808 | tf_op jit(solution)/shard_map/while/body/eval_jaxpr/bdv,bv->bd/dot_general | solution.py:54
  299.7 3.5 fusion.101
  309.7 6.8 broadcast_multiply_fusion.3
  316.5 27.0 %bitcast_dynamic-update-slice_fusion.4 = f32[4,2048,24,24]{3,2,1,0:T(8,128)} fusion(f32[4,2048,24,24]{3,2,1,0:T(8,128)} %get-tuple-element.346, s32[]{:T(128)} %get-tuple-element.345, bf16[2048,24,128]{2,0,1:T(8,128)(2,1)} %bitcast.212, bf16[2048,24,128]{2,0,1:T(8,128)(2,1)} %broadcast_multiply_fusion.3), kind=kOutput, calls=%fused_computation.3.clone.1 | convolution fusion | flops 301989888 | bytes 50332160 | tf_op jit(solution)/shard_map/while/body/eval_jaxpr/bdv,bev->bde/dot_general | solution.py:53
  343.5 20.8 %fusion.102 = f32[2048,1,24]{2,1,0:T(1,128)S(1)} fusion(bf16[2048,24,128]{2,0,1:T(8,128)(2,1)} %broadcast_multiply_fusion.3, bf16[2048,128,1]{1,0,2:T(8,128)(2,1)S(1)} %dynamic-slice_bitcast_fusion.5), kind=kOutput, calls=%fused_computation.7.clone.1 | convolution fusion | flops 12582912 | bytes 13303808 | tf_op jit(solution)/shard_map/while/body/eval_jaxpr/bdv,bv->bd/dot_general | solution.py:54
  365.6 3.5 fusion.101
  375.6 6.8 broadcast_multiply_fusion.3
  382.3 27.1 %bitcast_dynamic-update-slice_fusion.4 = f32[4,2048,24,24]{3,2,1,0:T(8,128)} fusion(f32[4,2048,24,24]{3,2,1,0:T(8,128)} %get-tuple-element.346, s32[]{:T(128)} %get-tuple-element.345, bf16[2048,24,128]{2,0,1:T(8,128)(2,1)} %bitcast.212, bf16[2048,24,128]{2,0,1:T(8,128)(2,1)} %broadcast_multiply_fusion.3), kind=kOutput, calls=%fused_computation.3.clone.1 | convolution fusion | flops 301989888 | bytes 50332160 | tf_op jit(solution)/shard_map/while/body/eval_jaxpr/bdv,bev->bde/dot_general | solution.py:53
  409.5 20.8 %fusion.102 = f32[2048,1,24]{2,1,0:T(1,128)S(1)} fusion(bf16[2048,24,128]{2,0,1:T(8,128)(2,1)} %broadcast_multiply_fusion.3, bf16[2048,128,1]{1,0,2:T(8,128)(2,1)S(1)} %dynamic-slice_bitcast_fusion.5), kind=kOutput, calls=%fused_computation.7.clone.1 | convolution fusion | flops 12582912 | bytes 13303808 | tf_op jit(solution)/shard_map/while/body/eval_jaxpr/bdv,bv->bd/dot_general | solution.py:54
  432.0 3.6 copy.267
  435.5 10.4 %reduce_sum.72 = f32[2048,24]{1,0:T(8,128)S(1)} reduce(f32[2048,4,24]{2,1,0:T(4,128)} %bitcast.215, f32[]{:T(128)} %constant.271.clone.1), dimensions={1}, to_apply=%region_3.4 | reduce | flops 147456 | bytes 983044 | tf_op jit(solution)/shard_map/reduce_sum | solution.py:108
  446.0 4.6 fusion.82
  450.6 5.6 copy.298
  456.2 5.5 copy.299
  461.7 5.5 copy.300
  467.2 5.5 copy.301
  472.7 5.5 copy.302
  478.3 4.3 copy.303
  482.6 3.4 copy.304
  486.0 3.8 copy.305
  493.2 10.1 %collective-permute-start.4 = (f32[3,17,1,5]{3,2,1,0:T(1,128)S(1)}, f32[3,17,1,5]{3,2,1,0:T(1,128)S(1)}, u32[]{:S(2)}, u32[]{:S(2)}) collective-permute-start(f32[3,17,1,5]{3,2,1,0:T(1,128)S(1)} %slice.627), channel_id=1, source_target_pairs={{0,1},{1,2},{2,3},{4,5},{5,6},{6,7},{8,9},{9,10},{10,11},{12,13},{... | collective-permute-start | bytes 3068 | tf_op jit(solution)/shard_map/ppermute | solution.py:27
  504.3 4.6 collective-permute-start.5
  508.9 41.1 %reduce_sum.74 = f32[2048,24,24]{2,1,0:T(8,128)} reduce(f32[2048,4,24,24]{3,2,1,0:T(8,128)} %bitcast.40, f32[]{:T(128)} %constant.271.clone.1), dimensions={1}, to_apply=%region_6.7 | reduce | flops 3538944 | bytes 23592964 | tf_op jit(solution)/shard_map/reduce_sum | solution.py:107
  552.4 3.8 collective-permute-done.6
  565.9 6.7 reshape.728
  572.8 14.2 %fusion.14 = f32[2048,24]{1,0:T(8,128)S(1)} fusion(f32[2048,24,24]{2,1,0:T(8,128)} %reduce_sum.74, f32[2048,24]{1,0:T(8,128)S(1)} %copy.307), kind=kLoop, calls=%fused_computation.24 | loop fusion | flops 2310144 | bytes 5111808
  601.5 4.7 collective-permute-start.8
  607.2 4.5 collective-permute-start.9
  614.4 42.1 %all-reduce.34 = (f32[]{:T(128)}, f32[]{:T(128)}) all-reduce(f32[]{:T(128)} %get-tuple-element.220, f32[]{:T(128)} %get-tuple-element.219), channel_id=1, replica_groups=mesh['gx'=8,'gy'=4] {'gx','gy'}, use_global_device_ids=true, to_apply=%region_5.6 | all-reduce | flops 2 | bytes 16 | tf_op jit(solution)/shard_map/psum | solution.py:143
  660.3 4.0 collective-permute-done.10
  674.0 6.7 reshape.729
  682.0 15.3 %fusion.15 = f32[2048,24]{1,0:T(8,128)} fusion(f32[2048,24,24]{2,1,0:T(8,128)} %reduce_sum.74, f32[2048,24]{1,0:T(8,128)} %copy.308), kind=kLoop, calls=%fused_computation.25 | loop fusion | flops 2310144 | bytes 5111808
  711.6 3.5 pad_add_fusion.1
  715.2 4.6 collective-permute-start.12
  730.0 42.7 %all-reduce.33 = (f32[]{:T(128)}, f32[]{:T(128)}) all-reduce(f32[]{:T(128)} %get-tuple-element.218, f32[]{:T(128)} %get-tuple-element.217), channel_id=1, replica_groups=mesh['gx'=8,'gy'=4] {'gx','gy'}, use_global_device_ids=true, to_apply=%region_10.11 | all-reduce | flops 2 | bytes 16 | tf_op jit(solution)/shard_map/psum | solution.py:143
  781.8 4.0 collective-permute-done.14
  795.6 7.2 reshape.730
  804.1 15.2 %fusion.16 = f32[2048,24]{1,0:T(8,128)} fusion(f32[2048,24,24]{2,1,0:T(8,128)} %reduce_sum.74, f32[2048,24]{1,0:T(8,128)S(1)} %copy.309), kind=kLoop, calls=%fused_computation.26 | loop fusion | flops 2310144 | bytes 5111808
  833.7 3.5 pad_add_fusion
  837.3 4.6 collective-permute-start.16
  850.2 41.9 %all-reduce.32 = (f32[]{:T(128)}, f32[]{:T(128)}) all-reduce(f32[]{:T(128)} %get-tuple-element.216, f32[]{:T(128)} %get-tuple-element.215), channel_id=1, replica_groups=mesh['gx'=8,'gy'=4] {'gx','gy'}, use_global_device_ids=true, to_apply=%region_14.15 | all-reduce | flops 2 | bytes 16 | tf_op jit(solution)/shard_map/psum | solution.py:143
  (202 shorter events, 165.8 us)
Async XLA Ops:
  0.6 12.1 %copy-start.6 = (s32[1,4096]{1,0:T(1,128)S(1)}, s32[1,4096]{1,0:T(1,128)}, u32[]{:S(2)}) copy-start(s32[1,4096]{1,0:T(1,128)} %param.30) | copy-start | bytes 49156
  0.6 12.2 %copy-start.5 = (s32[2,16,32,4]{2,3,1,0:T(4,128)S(1)}, s32[2,16,32,4]{2,3,1,0:T(4,128)}, u32[]{:S(2)}) copy-start(s32[2,16,32,4]{2,3,1,0:T(4,128)} %param.31) | copy-start | bytes 49156
  3.0 67.7 %collective-permute-start = (bf16[5,32,2048]{2,1,0:T(8,128)(2,1)}, bf16[5,32,2048]{2,1,0:T(8,128)(2,1)}, u32[]{:S(2)}, u32[]{:S(2)}) collective-permute-start(bf16[5,32,2048]{2,1,0:T(8,128)(2,1)} %get-tuple-element.249), channel_id=1, source_target_pairs={{0,4},{4,8},{8,12},{12,16},{16,20},{20,24},{24,28},{1,5},{5,9},{9,... | collective-permute-start | bytes 1966088 | tf_op jit(solution)/shard_map/ppermute | solution.py:18
  8.7 63.6 %collective-permute-start.1 = (bf16[5,32,2048]{2,1,0:T(8,128)(2,1)S(1)}, bf16[5,32,2048]{2,1,0:T(8,128)(2,1)}, u32[]{:S(2)}, u32[]{:S(2)}) collective-permute-start(bf16[5,32,2048]{2,1,0:T(8,128)(2,1)S(1)} %get-tuple-element.250), channel_id=1, source_target_pairs={{4,0},{8,4},{12,8},{16,12},{20,16},{24,20},{28,24},{5,1},{9,5},{13... | collective-permute-start | bytes 1966088 | tf_op jit(solution)/shard_map/ppermute | solution.py:19
  70.5 6.5 copy-start.1
  74.2 5.0 collective-permute-start.2
  75.5 5.5 collective-permute-start.3
  176.4 8.3 copy-start
  242.3 8.3 copy-start
  308.2 8.3 copy-start
  374.1 8.3 copy-start
  450.6 27.7 %copy-start.3 = (f32[3,2048]{0,1:T(8,128)S(1)}, f32[3,2048]{0,1:T(8,128)}, u32[]{:S(2)}) copy-start(f32[3,2048]{0,1:T(8,128)} %get-tuple-element.254) | copy-start | bytes 73732
  493.2 10.9 %collective-permute-start.4 = (f32[3,17,1,5]{3,2,1,0:T(1,128)S(1)}, f32[3,17,1,5]{3,2,1,0:T(1,128)S(1)}, u32[]{:S(2)}, u32[]{:S(2)}) collective-permute-start(f32[3,17,1,5]{3,2,1,0:T(1,128)S(1)} %slice.627), channel_id=1, source_target_pairs={{0,1},{1,2},{2,3},{4,5},{5,6},{6,7},{8,9},{9,10},{10,11},{12,13},{... | collective-permute-start | bytes 3068 | tf_op jit(solution)/shard_map/ppermute | solution.py:27
  504.3 45.8 %collective-permute-start.5 = (f32[3,1,32,5]{3,2,1,0:T(8,128)S(1)}, f32[3,1,32,5]{3,2,1,0:T(8,128)S(1)}, u32[]{:S(2)}, u32[]{:S(2)}) collective-permute-start(f32[3,1,32,5]{3,2,1,0:T(8,128)S(1)} %slice.630), channel_id=1, source_target_pairs={{0,4},{4,8},{8,12},{12,16},{16,20},{20,24},{24,28},{1,5},{5,9},{9,... | collective-permute-start | bytes 5768 | tf_op jit(solution)/shard_map/ppermute | solution.py:27
  550.2 6.0 collective-permute-start.6
  556.2 3.1 collective-permute-start.7
  601.5 5.5 collective-permute-start.8
  607.2 6.2 collective-permute-start.9
  658.0 6.2 collective-permute-start.10
  664.3 3.1 collective-permute-start.11
  715.2 5.6 collective-permute-start.12
  723.4 5.0 collective-permute-start.13
  729.1 47.4 %copy-start.2 = (f32[3,16,32,5]{3,2,1,0:T(8,128)}, f32[3,16,32,5]{3,2,1,0:T(8,128)S(1)}, u32[]{:S(2)}) copy-start(f32[3,16,32,5]{3,2,1,0:T(8,128)S(1)} %fusion.51) | copy-start | bytes 92164
  779.6 6.2 collective-permute-start.14
  785.9 3.1 collective-permute-start.15
  837.3 5.5 collective-permute-start.16
  842.9 0.9 copy-start.4
  843.8 4.7 collective-permute-start.17
where the time goes:
time: 914 us; the launch traced here: 903 us
  local copies, waits for them, and re-layouts  260 us (28%)
  other arithmetic  222 us (24%)
  matrix products  205 us (22%)
  blocking collectives  127 us (14%)
  starting transfers between devices  56.9 us (6%)
  waiting for transfers between devices  20.2 us (2%)
  between operations  11.3 us (1%)
    psum x3, blocking collectives, two_products(): lax.psum((jnp.sum(vector * vector), jnp.sum(vector * image)), ('gx', 'gy'))  127 us
    dot_general x4, matrix products, block_terms(): jnp.einsum('bdv,bev->bde', weighted, jacobian, preferred_element_type=jnp...  108 us
    dot_general x4, matrix products, block_terms(): jnp.einsum('bdv,bv->bd', weighted, resid_rows, preferred_element_type=jnp...  83.3 us
    squeeze x32, local copies, waits for them, and re-layouts, collect(): parts[node]  75.9 us
    unnamed x16, other arithmetic  51.3 us
    ppermute x14, starting transfers between devices, from_behind(): return lax.ppermute(block, axis, route)  47.1 us
    reduce_sum x1, other arithmetic, per_device(): elem_hess = hessian.reshape(elements, 4, 24, 24).sum(axis=1)  41.1 us
    scatter-add x1, other arithmetic, per_device(): jnp.zeros((local_blocks,), jnp.bfloat16).at[safe]  29.1 us
  transfers between devices with their start and end apart: 18, of which 13 were waited for; matrix products, arithmetic and copies ran while one was open for 13% of the time, Pallas kernels for 0%

commit v1 on v0

--- a/solution.py
+++ b/solution.py
@@ -2,6 +2,7 @@
 import jax.numpy as jnp
 from jax import lax
 from jax.sharding import PartitionSpec as P
+from jax.lax import psum
 
 BOUND = 4
 ITERS = 3
@@ -140,7 +141,15 @@
         return collect(images) + tikhonov * field
 
     def two_products(vector, image):
-        return lax.psum((jnp.sum(vector * vector), jnp.sum(vector * image)), ("gx", "gy"))
+
+        def remake_ways(in_array):
+            along_axis = "gx"
+            dev_axis = "gy"
+            for hop_no in (dev_axis, along_axis):
+                in_array = psum(in_array, hop_no)
+            return in_array
+
+        return remake_ways((jnp.sum(vector * vector), jnp.sum(vector * image)))
 
     rhs = collect(loads)
     increment = jnp.zeros_like(rhs)

time: 914 us -> 867 us (0.949)
  blocking collectives: 127 us -> 80.5 us
    psum x3 -> x6, blocking collectives: 127 us -> 80.5 us  [remake_ways(): in_array = psum(in_array, hop_no)]
  transfers between devices with their start and end apart: 18 -> 18, of which waited for: 13 -> 13; matrix products, arithmetic and copies ran while one was open for 13% -> 14% of each run, Pallas kernels for 0% -> 0%
where the time goes in v1:
time: 867 us; the launch traced here: 856 us
  local copies, waits for them, and re-layouts  260 us (30%)
  other arithmetic  222 us (26%)
  matrix products  205 us (24%)
  blocking collectives  80.5 us (9%)
  starting transfers between devices  56 us (6%)
  waiting for transfers between devices  19.8 us (2%)
  between operations  11.3 us (1%)
    dot_general x4, matrix products, block_terms(): jnp.einsum('bdv,bev->bde', weighted, jacobian, preferred_element_type=jnp...  108 us
    dot_general x4, matrix products, block_terms(): jnp.einsum('bdv,bv->bd', weighted, resid_rows, preferred_element_type=jnp...  83.3 us
    psum x6, blocking collectives, remake_ways(): in_array = psum(in_array, hop_no)  80.5 us
    squeeze x32, local copies, waits for them, and re-layouts, collect(): parts[node]  75.9 us
    unnamed x16, other arithmetic  51.3 us
    ppermute x14, starting transfers between devices, from_behind(): return lax.ppermute(block, axis, route)  46.2 us
    reduce_sum x1, other arithmetic, per_device(): elem_hess = hessian.reshape(elements, 4, 24, 24).sum(axis=1)  41.1 us
    scatter-add x1, other arithmetic, per_device(): jnp.zeros((local_blocks,), jnp.bfloat16).at[safe]  29.1 us
  transfers between devices with their start and end apart: 18, of which 13 were waited for; matrix products, arithmetic and copies ran while one was open for 14% of the time, Pallas kernels for 0%

profile of v1, /device:TPU:0, one launch (start us, length us, event | category | flops | bytes accessed | tf_op | source)
XLA Modules:
  0.0 856.3 jit_solution(14259471021052187652)
XLA Ops:
  3.0 5.7 collective-permute-start
  13.6 4.5 reshape.733
  18.1 4.5 reshape.734
  22.7 4.0 convert_element_type.286
  26.6 4.2 convert_element_type.287
  30.8 29.1 %scatter_custom_fusion = bf16[8192]{0:T(1024)(128)(2,1)S(1)} fusion(s32[4096]{0:T(1024)S(1)} %bitcast.232, bf16[4096]{0:T(1024)(128)(2,1)S(1)} %fusion.63, bf16[]{:T(256)} %constant.278.clone.1), kind=kCustom, calls=%fused_computation.157 | custom fusion | flops 4096 | bytes 16386 | tf_op jit(solution)/shard_map/scatter-add | solution.py:103
  59.9 10.5 %reshape.725 = bf16[3,8192,128]{2,1,0:T(8,128)(2,1)} reshape(bf16[3,16,32,2048]{3,2,1,0:T(8,128)(2,1)} %param.26) | data formatting | bytes 12582912 | tf_op jit(solution)/shard_map/reshape | solution.py:96
  81.0 6.1 pad_maximum_fusion
  87.1 4.8 copy.263
  91.9 10.6 %reshape.727 = bf16[1092,4,512]{2,1,0:T(4,128)(2,1)} reshape(bf16[26,42,2048]{2,1,0:T(8,128)(2,1)} %copy.263) | data formatting | bytes 8945664 | tf_op jit(solution)/shard_map/reshape | solution.py:82
  102.4 26.4 %gather_fusion = bf16[2048,512]{1,0:T(8,128)(2,1)S(1)} fusion(bf16[1092,4,512]{2,1,0:T(4,128)(2,1)} %reshape.727, s32[2048]{0:T(1024)S(1)} %reshape.737), kind=kCustom, calls=%fused_computation | custom fusion | bytes 4210688 | tf_op jit(solution)/shard_map/gather | solution.py:87
  131.7 26.4 %gather_fusion.1 = bf16[2048,512]{1,0:T(8,128)(2,1)S(1)} fusion(bf16[1092,4,512]{2,1,0:T(4,128)(2,1)} %reshape.727, s32[2048]{0:T(1024)S(1)} %reshape.743), kind=kCustom, calls=%fused_computation.1 | custom fusion | bytes 4210688 | tf_op jit(solution)/shard_map/gather | solution.py:88
  161.0 6.7 subtract_convert_fusion
  167.7 264.3 %while.20 = (s32[]{:T(128)}, f32[4,2048,24,24]{3,2,1,0:T(8,128)}, f32[4,2048,24]{1,2,0:T(8,128)}, s32[4,2048]{1,0:T(4,128)S(1)}, f32[4,8,128]{2,0,1:T(4,128)S(1)...) while((s32[]{:T(128)}, f32[4,2048,24,24]{3,2,1,0:T(8,128)}, ...), condition=%wide.region_2.3_spmd, body=%wide.region_1.2_spmd.sunk | while | flops 434905088 | bytes 179807376 | solution.py:68
  167.9 3.5 fusion.101
  177.9 6.8 broadcast_multiply_fusion.3
  184.7 27.1 %bitcast_dynamic-update-slice_fusion.4 = f32[4,2048,24,24]{3,2,1,0:T(8,128)} fusion(f32[4,2048,24,24]{3,2,1,0:T(8,128)} %get-tuple-element.352, s32[]{:T(128)} %get-tuple-element.351, bf16[2048,24,128]{2,0,1:T(8,128)(2,1)} %bitcast.212, bf16[2048,24,128]{2,0,1:T(8,128)(2,1)} %broadcast_multiply_fusion.3), kind=kOutput, calls=%fused_computation.3.clone.1 | convolution fusion | flops 301989888 | bytes 50332160 | tf_op jit(solution)/shard_map/while/body/eval_jaxpr/bdv,bev->bde/dot_general | solution.py:54
  211.8 20.8 %fusion.102 = f32[2048,1,24]{2,1,0:T(1,128)S(1)} fusion(bf16[2048,24,128]{2,0,1:T(8,128)(2,1)} %broadcast_multiply_fusion.3, bf16[2048,128,1]{1,0,2:T(8,128)(2,1)S(1)} %dynamic-slice_bitcast_fusion.5), kind=kOutput, calls=%fused_computation.7.clone.1 | convolution fusion | flops 12582912 | bytes 13303808 | tf_op jit(solution)/shard_map/while/body/eval_jaxpr/bdv,bv->bd/dot_general | solution.py:55
  233.8 3.5 fusion.101
  243.8 6.8 broadcast_multiply_fusion.3
  250.6 27.0 %bitcast_dynamic-update-slice_fusion.4 = f32[4,2048,24,24]{3,2,1,0:T(8,128)} fusion(f32[4,2048,24,24]{3,2,1,0:T(8,128)} %get-tuple-element.352, s32[]{:T(128)} %get-tuple-element.351, bf16[2048,24,128]{2,0,1:T(8,128)(2,1)} %bitcast.212, bf16[2048,24,128]{2,0,1:T(8,128)(2,1)} %broadcast_multiply_fusion.3), kind=kOutput, calls=%fused_computation.3.clone.1 | convolution fusion | flops 301989888 | bytes 50332160 | tf_op jit(solution)/shard_map/while/body/eval_jaxpr/bdv,bev->bde/dot_general | solution.py:54
  277.7 20.8 %fusion.102 = f32[2048,1,24]{2,1,0:T(1,128)S(1)} fusion(bf16[2048,24,128]{2,0,1:T(8,128)(2,1)} %broadcast_multiply_fusion.3, bf16[2048,128,1]{1,0,2:T(8,128)(2,1)S(1)} %dynamic-slice_bitcast_fusion.5), kind=kOutput, calls=%fused_computation.7.clone.1 | convolution fusion | flops 12582912 | bytes 13303808 | tf_op jit(solution)/shard_map/while/body/eval_jaxpr/bdv,bv->bd/dot_general | solution.py:55
  299.7 3.5 fusion.101
  309.7 6.8 broadcast_multiply_fusion.3
  316.5 27.0 %bitcast_dynamic-update-slice_fusion.4 = f32[4,2048,24,24]{3,2,1,0:T(8,128)} fusion(f32[4,2048,24,24]{3,2,1,0:T(8,128)} %get-tuple-element.352, s32[]{:T(128)} %get-tuple-element.351, bf16[2048,24,128]{2,0,1:T(8,128)(2,1)} %bitcast.212, bf16[2048,24,128]{2,0,1:T(8,128)(2,1)} %broadcast_multiply_fusion.3), kind=kOutput, calls=%fused_computation.3.clone.1 | convolution fusion | flops 301989888 | bytes 50332160 | tf_op jit(solution)/shard_map/while/body/eval_jaxpr/bdv,bev->bde/dot_general | solution.py:54
  343.5 20.8 %fusion.102 = f32[2048,1,24]{2,1,0:T(1,128)S(1)} fusion(bf16[2048,24,128]{2,0,1:T(8,128)(2,1)} %broadcast_multiply_fusion.3, bf16[2048,128,1]{1,0,2:T(8,128)(2,1)S(1)} %dynamic-slice_bitcast_fusion.5), kind=kOutput, calls=%fused_computation.7.clone.1 | convolution fusion | flops 12582912 | bytes 13303808 | tf_op jit(solution)/shard_map/while/body/eval_jaxpr/bdv,bv->bd/dot_general | solution.py:55
  365.6 3.5 fusion.101
  375.6 6.8 broadcast_multiply_fusion.3
  382.3 27.1 %bitcast_dynamic-update-slice_fusion.4 = f32[4,2048,24,24]{3,2,1,0:T(8,128)} fusion(f32[4,2048,24,24]{3,2,1,0:T(8,128)} %get-tuple-element.352, s32[]{:T(128)} %get-tuple-element.351, bf16[2048,24,128]{2,0,1:T(8,128)(2,1)} %bitcast.212, bf16[2048,24,128]{2,0,1:T(8,128)(2,1)} %broadcast_multiply_fusion.3), kind=kOutput, calls=%fused_computation.3.clone.1 | convolution fusion | flops 301989888 | bytes 50332160 | tf_op jit(solution)/shard_map/while/body/eval_jaxpr/bdv,bev->bde/dot_general | solution.py:54
  409.5 20.8 %fusion.102 = f32[2048,1,24]{2,1,0:T(1,128)S(1)} fusion(bf16[2048,24,128]{2,0,1:T(8,128)(2,1)} %broadcast_multiply_fusion.3, bf16[2048,128,1]{1,0,2:T(8,128)(2,1)S(1)} %dynamic-slice_bitcast_fusion.5), kind=kOutput, calls=%fused_computation.7.clone.1 | convolution fusion | flops 12582912 | bytes 13303808 | tf_op jit(solution)/shard_map/while/body/eval_jaxpr/bdv,bv->bd/dot_general | solution.py:55
  432.0 3.6 copy.267
  435.5 10.4 %reduce_sum.72 = f32[2048,24]{1,0:T(8,128)S(1)} reduce(f32[2048,4,24]{2,1,0:T(4,128)} %bitcast.215, f32[]{:T(128)} %constant.271.clone.1), dimensions={1}, to_apply=%region_3.4 | reduce | flops 147456 | bytes 983044 | tf_op jit(solution)/shard_map/reduce_sum | solution.py:109
  446.0 4.6 fusion.82
  450.6 5.6 copy.298
  456.2 5.5 copy.299
  461.7 5.5 copy.300
  467.2 5.5 copy.301
  472.7 5.5 copy.302
  478.3 4.3 copy.303
  486.0 3.8 copy.305
  493.2 10.1 %collective-permute-start.4 = (f32[3,17,1,5]{3,2,1,0:T(1,128)S(1)}, f32[3,17,1,5]{3,2,1,0:T(1,128)S(1)}, u32[]{:S(2)}, u32[]{:S(2)}) collective-permute-start(f32[3,17,1,5]{3,2,1,0:T(1,128)S(1)} %slice.627), channel_id=1, source_target_pairs={{0,1},{1,2},{2,3},{4,5},{5,6},{6,7},{8,9},{9,10},{10,11},{12,13},{... | collective-permute-start | bytes 3068 | tf_op jit(solution)/shard_map/ppermute | solution.py:28
  504.3 4.6 collective-permute-start.5
  508.9 41.1 %reduce_sum.74 = f32[2048,24,24]{2,1,0:T(8,128)} reduce(f32[2048,4,24,24]{3,2,1,0:T(8,128)} %bitcast.40, f32[]{:T(128)} %constant.271.clone.1), dimensions={1}, to_apply=%region_7.8 | reduce | flops 3538944 | bytes 23592964 | tf_op jit(solution)/shard_map/reduce_sum | solution.py:108
  552.4 3.8 collective-permute-done.6
  565.9 6.7 reshape.728
  572.8 14.2 %fusion.14 = f32[2048,24]{1,0:T(8,128)S(1)} fusion(f32[2048,24,24]{2,1,0:T(8,128)} %reduce_sum.74, f32[2048,24]{1,0:T(8,128)S(1)} %copy.307), kind=kLoop, calls=%fused_computation.24 | loop fusion | flops 2310144 | bytes 5111808
  601.5 4.7 collective-permute-start.8
  607.2 4.5 collective-permute-start.9
  614.4 6.5 all-reduce.37
  620.8 21.0 %all-reduce.34 = (f32[]{:T(128)}, f32[]{:T(128)}) all-reduce(f32[]{:T(128)} %get-tuple-element.247, f32[]{:T(128)} %get-tuple-element.248), channel_id=1, replica_groups=mesh['gx'=8,'gy'=4] {'gx'}, use_global_device_ids=true, to_apply=%region_6.7 | all-reduce | flops 2 | bytes 16 | tf_op jit(solution)/shard_map/psum | solution.py:149
  645.6 3.8 collective-permute-done.10
  659.1 6.8 reshape.729
  667.2 15.3 %fusion.15 = f32[2048,24]{1,0:T(8,128)} fusion(f32[2048,24,24]{2,1,0:T(8,128)} %reduce_sum.74, f32[2048,24]{1,0:T(8,128)} %copy.308), kind=kLoop, calls=%fused_computation.25 | loop fusion | flops 2310144 | bytes 5111808
  696.9 3.5 pad_add_fusion.1
  700.4 4.6 collective-permute-start.12
  715.1 6.3 all-reduce.36
  721.5 20.1 %all-reduce.33 = (f32[]{:T(128)}, f32[]{:T(128)}) all-reduce(f32[]{:T(128)} %get-tuple-element.245, f32[]{:T(128)} %get-tuple-element.246), channel_id=1, replica_groups=mesh['gx'=8,'gy'=4] {'gx'}, use_global_device_ids=true, to_apply=%region_13.14 | all-reduce | flops 2 | bytes 16 | tf_op jit(solution)/shard_map/psum | solution.py:149
  750.8 3.8 collective-permute-done.14
  764.2 7.4 reshape.730
  772.9 15.2 %fusion.16 = f32[2048,24]{1,0:T(8,128)} fusion(f32[2048,24,24]{2,1,0:T(8,128)} %reduce_sum.74, f32[2048,24]{1,0:T(8,128)S(1)} %copy.309), kind=kLoop, calls=%fused_computation.26 | loop fusion | flops 2310144 | bytes 5111808
  802.6 3.5 pad_add_fusion
  806.1 4.6 collective-permute-start.16
  818.5 6.5 all-reduce.35
  825.0 20.1 %all-reduce.32 = (f32[]{:T(128)}, f32[]{:T(128)}) all-reduce(f32[]{:T(128)} %get-tuple-element.243, f32[]{:T(128)} %get-tuple-element.244), channel_id=1, replica_groups=mesh['gx'=8,'gy'=4] {'gx'}, use_global_device_ids=true, to_apply=%region_19.20 | all-reduce | flops 2 | bytes 16 | tf_op jit(solution)/shard_map/psum | solution.py:149
  (205 shorter events, 175.3 us)
Async XLA Ops:
  0.6 12.1 %copy-start.6 = (s32[1,4096]{1,0:T(1,128)S(1)}, s32[1,4096]{1,0:T(1,128)}, u32[]{:S(2)}) copy-start(s32[1,4096]{1,0:T(1,128)} %param.30) | copy-start | bytes 49156
  0.6 12.2 %copy-start.5 = (s32[2,16,32,4]{2,3,1,0:T(4,128)S(1)}, s32[2,16,32,4]{2,3,1,0:T(4,128)}, u32[]{:S(2)}) copy-start(s32[2,16,32,4]{2,3,1,0:T(4,128)} %param.31) | copy-start | bytes 49156
  3.0 67.7 %collective-permute-start = (bf16[5,32,2048]{2,1,0:T(8,128)(2,1)}, bf16[5,32,2048]{2,1,0:T(8,128)(2,1)}, u32[]{:S(2)}, u32[]{:S(2)}) collective-permute-start(bf16[5,32,2048]{2,1,0:T(8,128)(2,1)} %get-tuple-element.255), channel_id=1, source_target_pairs={{0,4},{4,8},{8,12},{12,16},{16,20},{20,24},{24,28},{1,5},{5,9},{9,... | collective-permute-start | bytes 1966088 | tf_op jit(solution)/shard_map/ppermute | solution.py:19
  8.7 63.6 %collective-permute-start.1 = (bf16[5,32,2048]{2,1,0:T(8,128)(2,1)S(1)}, bf16[5,32,2048]{2,1,0:T(8,128)(2,1)}, u32[]{:S(2)}, u32[]{:S(2)}) collective-permute-start(bf16[5,32,2048]{2,1,0:T(8,128)(2,1)S(1)} %get-tuple-element.256), channel_id=1, source_target_pairs={{4,0},{8,4},{12,8},{16,12},{20,16},{24,20},{28,24},{5,1},{9,5},{13... | collective-permute-start | bytes 1966088 | tf_op jit(solution)/shard_map/ppermute | solution.py:20
  70.5 6.5 copy-start.1
  74.2 5.0 collective-permute-start.2
  75.5 5.5 collective-permute-start.3
  176.4 8.3 copy-start
  242.3 8.3 copy-start
  308.2 8.3 copy-start
  374.1 8.3 copy-start
  450.6 27.7 %copy-start.3 = (f32[3,2048]{0,1:T(8,128)S(1)}, f32[3,2048]{0,1:T(8,128)}, u32[]{:S(2)}) copy-start(f32[3,2048]{0,1:T(8,128)} %get-tuple-element.260) | copy-start | bytes 73732
  493.2 10.9 %collective-permute-start.4 = (f32[3,17,1,5]{3,2,1,0:T(1,128)S(1)}, f32[3,17,1,5]{3,2,1,0:T(1,128)S(1)}, u32[]{:S(2)}, u32[]{:S(2)}) collective-permute-start(f32[3,17,1,5]{3,2,1,0:T(1,128)S(1)} %slice.627), channel_id=1, source_target_pairs={{0,1},{1,2},{2,3},{4,5},{5,6},{6,7},{8,9},{9,10},{10,11},{12,13},{... | collective-permute-start | bytes 3068 | tf_op jit(solution)/shard_map/ppermute | solution.py:28
  504.3 45.8 %collective-permute-start.5 = (f32[3,1,32,5]{3,2,1,0:T(8,128)S(1)}, f32[3,1,32,5]{3,2,1,0:T(8,128)S(1)}, u32[]{:S(2)}, u32[]{:S(2)}) collective-permute-start(f32[3,1,32,5]{3,2,1,0:T(8,128)S(1)} %slice.630), channel_id=1, source_target_pairs={{0,4},{4,8},{8,12},{12,16},{16,20},{20,24},{24,28},{1,5},{5,9},{9,... | collective-permute-start | bytes 5768 | tf_op jit(solution)/shard_map/ppermute | solution.py:28
  550.2 6.0 collective-permute-start.6
  556.2 3.1 collective-permute-start.7
  601.5 5.5 collective-permute-start.8
  607.2 6.2 collective-permute-start.9
  643.4 6.0 collective-permute-start.10
  649.4 3.1 collective-permute-start.11
  700.4 5.6 collective-permute-start.12
  708.6 4.7 collective-permute-start.13
  714.1 31.4 %copy-start.2 = (f32[3,16,32,5]{3,2,1,0:T(8,128)}, f32[3,16,32,5]{3,2,1,0:T(8,128)S(1)}, u32[]{:S(2)}) copy-start(f32[3,16,32,5]{3,2,1,0:T(8,128)S(1)} %fusion.51) | copy-start | bytes 92164
  748.5 6.0 collective-permute-start.14
  754.5 3.1 collective-permute-start.15
  806.1 5.4 collective-permute-start.16
  811.7 0.9 copy-start.4
  812.6 4.2 collective-permute-start.17
